TPU v7x, 512 devices: a whole 4x8x8 slice. The times are simulated.
512 devices in a mesh: blk: 32 (over x_lo, y, core), tm: 16 (over z, x_hi).
Axes of the slice: x: 4 (x_hi: 2, x_lo: 2; x = x_hi * 2 + x_lo), y: 8, z: 8, core: 2. Of those that a mesh axis runs over, the one named last changes fastest.
Arguments:
- clips: bfloat16 [32, 32, 16, 36, 256], P('blk', 'tm'), may hold values from -6 to 6
- cotangent: bfloat16 [32, 32, 16, 36, 256], P('blk', 'tm'), may hold values from -6 to 6
- conv_master: float32 [3072, 256], P('blk'), may hold values from -0.125 to 0.125
- first_moment: float32 [3072, 256], P('blk'), may hold values from -3 to 3
- second_moment: float32 [3072, 256], P('blk'), may hold values from 0.1 to 100
- norm_gain: float32 [256], replicated, may hold values from 0.5 to 1.5
- norm_bias: float32 [256], replicated, may hold values from -3 to 3
Outputs:
- block_out: bfloat16 [32, 32, 16, 36, 256], P('blk', 'tm')
- input_grad: bfloat16 [32, 32, 16, 36, 256], P('blk', 'tm')
- new_master: float32 [3072, 256], P('blk')
- new_first: float32 [3072, 256], P('blk')
- new_second: float32 [3072, 256], P('blk')
- norm_grads: float32 [2, 256], replicated
All inputs are finite; a program needn't handle non-finite values.
Results may differ from a plain program's by a relative error of at most 0.0063.
Values may be sent and summed in bfloat16 or wider, within the bound.
A program may use at most 64 MiB of HBM per device.

v0:
```python
import jax
import jax.numpy as jnp
from jax import lax
from jax.sharding import PartitionSpec as P

GROUPS = 32
beta_one = 0.9
beta_two = 0.999
learn_rate = 0.003
adam_eps = 1e-08
bias_first = 1.0 - 0.9**10
bias_second = 1.0 - 0.999**10


def extended(block, sides, width):
    for axis, dim in sides:
        count = lax.axis_size(axis)
        forward = [(i, i + 1) for i in range(count - 1)]
        backward = [(target, source) for source, target in forward]
        low = lax.ppermute(
            lax.slice_in_dim(block, block.shape[dim] - width, None, axis=dim), axis, forward
        )
        high = lax.ppermute(lax.slice_in_dim(block, 0, width, axis=dim), axis, backward)
        block = jnp.concatenate([low, block, high], axis=dim)
    return block


def norm_act(field, gain, bias):
    shape = field.shape
    grouped = field.reshape(shape[:-3] + (shape[-3] * shape[-2], GROUPS, shape[-1] // GROUPS))
    center = jnp.mean(grouped, axis=(-3, -1), keepdims=True)
    spread = jnp.mean((grouped - center) ** 2, axis=(-3, -1), keepdims=True)
    normed = ((grouped - center) * lax.rsqrt(spread + 1e-05)).reshape(shape)
    return jax.nn.silu(normed * gain + bias)


def adam_update(gradient, master, first, second):
    new_first = beta_one * first + (1.0 - beta_one) * gradient
    new_second = beta_two * second + (1.0 - beta_two) * gradient * gradient
    update = new_first / bias_first / (jnp.sqrt(new_second / bias_second) + adam_eps)
    return (master - learn_rate * update, new_first, new_second)


def shards(clips, cotangent, conv_master, first_moment, second_moment, norm_gain, norm_bias):
    f32 = jnp.float32
    frames, height, width, channels = (
        clips.shape[1],
        clips.shape[2],
        clips.shape[3],
        clips.shape[4],
    )
    weights = lax.all_gather(conv_master.astype(jnp.bfloat16), "blk", axis=0, tiled=True)
    inputs32 = clips.astype(f32)
    act32, pullback = jax.vjp(norm_act, inputs32, norm_gain, norm_bias)
    act = act32.astype(jnp.bfloat16)
    act_padded = jnp.pad(act, ((0, 0), (0, 0), (1, 1), (1, 1), (0, 0)))
    space32 = jnp.zeros(clips.shape, f32)
    for row_tap in range(3):
        for col_tap in range(3):
            tap_index = 3 * row_tap + col_tap
            window = act_padded[:, :, row_tap : row_tap + height, col_tap : col_tap + width, :]
            tap = weights[tap_index * channels : (tap_index + 1) * channels]
            space32 = space32 + jnp.einsum(
                "bfhwc,cd->bfhwd", window, tap, preferred_element_type=f32
            )
    space = space32.astype(jnp.bfloat16)
    space_padded = extended(space, (("tm", 1),), 1)
    temporal = jnp.zeros(clips.shape, f32)
    for frame_tap in range(3):
        tap = weights[(9 + frame_tap) * channels : (10 + frame_tap) * channels]
        temporal = temporal + jnp.einsum(
            "bfhwc,cd->bfhwd",
            space_padded[:, frame_tap : frame_tap + frames],
            tap,
            preferred_element_type=f32,
        )
    block_out = (inputs32 + temporal).astype(jnp.bfloat16)
    back_weights = lax.all_gather(conv_master.astype(jnp.bfloat16), "blk", axis=0, tiled=True)
    grad_padded = extended(cotangent, (("tm", 1),), 1)
    space_grad32 = jnp.zeros(clips.shape, f32)
    temporal_grads = []
    for frame_tap in range(3):
        tap = back_weights[(9 + frame_tap) * channels : (10 + frame_tap) * channels]
        space_grad32 = space_grad32 + jnp.einsum(
            "bfhwd,cd->bfhwc",
            grad_padded[:, 2 - frame_tap : 2 - frame_tap + frames],
            tap,
            preferred_element_type=f32,
        )
        temporal_grads.append(
            jnp.einsum(
                "bfhwc,bfhwd->cd",
                space_padded[:, frame_tap : frame_tap + frames],
                cotangent,
                preferred_element_type=f32,
            )
        )
    space_grad = space_grad32.astype(jnp.bfloat16)
    sgrad_padded = jnp.pad(space_grad, ((0, 0), (0, 0), (1, 1), (1, 1), (0, 0)))
    act_grad = jnp.zeros(clips.shape, f32)
    spatial_grads = []
    for row_tap in range(3):
        for col_tap in range(3):
            tap_index = 3 * row_tap + col_tap
            tap = back_weights[tap_index * channels : (tap_index + 1) * channels]
            window = act_padded[:, :, row_tap : row_tap + height, col_tap : col_tap + width, :]
            spatial_grads.append(
                jnp.einsum("bfhwc,bfhwd->cd", window, space_grad, preferred_element_type=f32)
            )
            back_window = sgrad_padded[
                :, :, 2 - row_tap : 2 - row_tap + height, 2 - col_tap : 2 - col_tap + width, :
            ]
            act_grad = act_grad + jnp.einsum(
                "bfhwd,cd->bfhwc", back_window, tap, preferred_element_type=f32
            )
    input_term, gain_grad, bias_grad = pullback(act_grad)
    input_grad = (cotangent.astype(f32) + input_term).astype(jnp.bfloat16)
    local_gradient = jnp.concatenate(spatial_grads + temporal_grads, axis=0)
    norm_grads = lax.psum(jnp.stack([gain_grad, bias_grad]), ("blk", "tm"))
    row_block = lax.psum_scatter(local_gradient, "blk", scatter_dimension=0, tiled=True)
    gradient = lax.psum(row_block, "tm")
    new_master, new_first, new_second = adam_update(
        gradient, conv_master, first_moment, second_moment
    )
    return (block_out, input_grad, new_master, new_first, new_second, norm_grads)


def solution(mesh):
    placed = (
        P("blk", "tm", None, None, None),
        P("blk", "tm", None, None, None),
        P("blk", None),
        P("blk", None),
        P("blk", None),
        P(),
        P(),
    )
    return jax.shard_map(
        shards,
        mesh=mesh,
        in_specs=placed,
        out_specs=(
            P("blk", "tm", None, None, None),
            P("blk", "tm", None, None, None),
            P("blk", None),
            P("blk", None),
            P("blk", None),
            P(),
        ),
        check_vma=False,
    )
```

profile of v0, /device:TPU:8, one launch (start us, length us, event | category | flops | bytes accessed | tf_op | source)
XLA Modules:
  0.0 426.8 jit_solution(4757618439813596500)
XLA Ops:
  7.2 1.5 convert_element_type.38
  8.8 1.3 copy.26
  10.1 0.8 fusion.179
  10.9 4.9 %collective-permute-start.3 = (bf16[1,1,16,36,256]{4,3,2,1,0:T(8,128)(2,1)S(1)}, bf16[1,1,16,36,256]{4,3,2,1,0:T(8,128)(2,1)S(1)}, u32[]{:S(2)}, u32[]{:S(2)}) collective-permute-start(bf16[1,1,16,36,256]{4,3,2,1,0:T(8,128)(2,1)S(1)} %get-tuple-element.25), channel_id=1, source_target_pairs={{0,1},{1,2},{2,3},{3,4},{4,5},{5,6},{6,7},{7,8},{8,9},{9,10},{10,1... | collective-permute-start | bytes 884744 | tf_op jit(solution)/shard_map/ppermute | solution.py:20
  15.8 1.3 collective-permute-start.2
  18.3 11.4 %collective-permute-done.3 = bf16[1,1,16,36,256]{4,3,2,1,0:T(8,128)(2,1)S(1)} collective-permute-done((bf16[1,1,16,36,256]{4,3,2,1,0:T(8,128)(2,1)S(1)}, bf16[1,1,16,36,256]{4,3,2,1,0:T(8,128)(2,1)S(1)}, u32[]{:S(2)}, u32[]{:S(2)}) %collective-permute-start.3) | collective-permute-done | bytes 294944 | tf_op jit(solution)/shard_map/ppermute | solution.py:20
  29.8 0.7 copy-done.12
  30.5 50.4 %all-gather.2.cloned.1.call-done = bf16[3072,256]{1,0:T(8,128)(2,1)} async-done(((bf16[96,256]{1,0:T(8,128)(2,1)}), bf16[3072,256]{1,0:T(8,128)(2,1)}) %all-gather.2.cloned.1.call-update) | async-done | bytes 1572880 | tf_op jit(solution)/shard_map/all_gather | solution.py:52
  80.9 1.5 fusion.51
  82.5 0.4 fusion.114
  82.9 1.4 fusion.9
  84.3 0.4 fusion.66
  85.1 0.4 convolution_add_fusion.6
  85.5 0.4 convolution_add_fusion.5
  86.3 0.4 convolution_add_fusion.3
  86.7 0.4 convolution_add_fusion.2
  87.8 1.2 fusion.26
  89.0 1.1 copy-done.5
  90.1 0.5 fusion.37
  91.7 3.0 fusion.14
  94.7 1.1 fusion.49
  95.8 1.1 fusion.48
  96.9 1.1 fusion.47
  98.0 1.1 fusion.46
  99.1 1.1 fusion.45
  100.2 1.1 fusion.44
  101.3 1.1 fusion.43
  103.5 0.4 convolution_add_fusion.15
  105.0 0.5 convolution_add_fusion.11
  106.0 5.0 %collective-permute-start = (bf16[1,1,16,36,256]{4,3,2,1,0:T(8,128)(2,1)S(1)}, bf16[1,1,16,36,256]{4,3,2,1,0:T(8,128)(2,1)S(1)}, u32[]{:S(2)}, u32[]{:S(2)}) collective-permute-start(bf16[1,1,16,36,256]{4,3,2,1,0:T(8,128)(2,1)S(1)} %get-tuple-element.26), channel_id=1, source_target_pairs={{0,1},{1,2},{2,3},{3,4},{4,5},{5,6},{6,7},{7,8},{8,9},{9,10},{10,1... | collective-permute-start | bytes 884744 | tf_op jit(solution)/shard_map/ppermute | solution.py:20
  111.0 1.1 fusion.42
  112.1 1.4 collective-permute-start.1
  113.5 1.1 fusion.41
  114.6 10.7 %collective-permute-done = bf16[1,1,16,36,256]{4,3,2,1,0:T(8,128)(2,1)S(1)} collective-permute-done((bf16[1,1,16,36,256]{4,3,2,1,0:T(8,128)(2,1)S(1)}, bf16[1,1,16,36,256]{4,3,2,1,0:T(8,128)(2,1)S(1)}, u32[]{:S(2)}, u32[]{:S(2)}) %collective-permute-start) | collective-permute-done | bytes 294944 | tf_op jit(solution)/shard_map/ppermute | solution.py:20
  125.3 1.2 fusion.40
  126.5 1.1 fusion.39
  127.7 0.7 copy-done.10
  128.4 1.2 fusion.38
  129.7 1.0 copy-done.6
  130.7 0.9 copy.36
  131.7 98.4 %psum.15 = f32[2,256]{1,0:T(2,128)} all-reduce(f32[2,256]{1,0:T(2,128)S(1)} %pad_maximum_fusion.4), channel_id=1, replica_groups=mesh['blk'=32,'tm'=16] {'blk','tm'}, use_global_device_ids=true, to_apply=%region_14.15 | all-reduce | flops 512 | bytes 4096 | tf_op jit(solution)/shard_map/psum | solution.py:119
  230.1 1.4 fusion.129
  231.6 1.4 fusion.127
  233.0 19.1 %reduce-scatter.2.cloned.1.call-done = f32[96,256]{1,0:T(8,128)} async-done(((f32[3072,256]{1,0:T(8,128)}), f32[96,256]{1,0:T(8,128)}) %reduce-scatter.2.cloned.1.call-update) | async-done | bytes 98320 | tf_op jit(solution)/shard_map/reduce_scatter | solution.py:120
  252.1 2.2 fusion.11
  254.4 0.9 copy.35
  255.3 163.4 %all-reduce.4.cloned.1.call-done = f32[96,256]{1,0:T(8,128)} async-done(((f32[96,256]{1,0:T(8,128)}), f32[96,256]{1,0:T(8,128)}) %all-reduce.4.cloned.1.call-update) | async-done | bytes 98320 | tf_op jit(solution)/shard_map/psum | solution.py:121
  418.7 1.6 multiply_subtract_fusion
  (75 shorter events, 6.7 us)
Async XLA Ops:
  7.2 73.8 %all-gather.2.cloned.1.call-start = ((), (), s32[]{:S(2)}) async-start(), calls=%async_computation.1 | async-start | bytes 1622016 | tf_op jit(solution)/shard_map/all_gather | solution.py:52
  8.7 8.4 %copy-start = (bf16[1,2,16,36,256]{4,2,3,1,0:T(8,128)(2,1)S(1)}, bf16[1,2,16,36,256]{4,2,3,1,0:T(8,128)(2,1)}, u32[]{:S(2)}) copy-start(bf16[1,2,16,36,256]{4,2,3,1,0:T(8,128)(2,1)} %param.7) | copy-start | bytes 1769476
  8.8 243.3 %reduce-scatter.2.cloned.1.call-start = ((), (), s32[]{:S(2)}) async-start(), calls=%async_computation.2 | async-start | bytes 3244032 | tf_op jit(solution)/shard_map/reduce_scatter | solution.py:120
  10.9 18.9 %collective-permute-start.3 = (bf16[1,1,16,36,256]{4,3,2,1,0:T(8,128)(2,1)S(1)}, bf16[1,1,16,36,256]{4,3,2,1,0:T(8,128)(2,1)S(1)}, u32[]{:S(2)}, u32[]{:S(2)}) collective-permute-start(bf16[1,1,16,36,256]{4,3,2,1,0:T(8,128)(2,1)S(1)} %get-tuple-element.25), channel_id=1, source_target_pairs={{0,1},{1,2},{2,3},{3,4},{4,5},{5,6},{6,7},{7,8},{8,9},{9,10},{10,1... | collective-permute-start | bytes 884744 | tf_op jit(solution)/shard_map/ppermute | solution.py:20
  15.8 67.1 %collective-permute-start.2 = (bf16[1,1,16,36,256]{4,3,2,1,0:T(8,128)(2,1)}, bf16[1,1,16,36,256]{4,3,2,1,0:T(8,128)(2,1)}, u32[]{:S(2)}, u32[]{:S(2)}) collective-permute-start(bf16[1,1,16,36,256]{4,3,2,1,0:T(8,128)(2,1)} %get-tuple-element.24), channel_id=1, source_target_pairs={{1,0},{2,1},{3,2},{4,3},{5,4},{6,5},{7,6},{8,7},{9,8},{10,9},{11,1... | collective-permute-start | bytes 884744 | tf_op jit(solution)/shard_map/ppermute | solution.py:23
  17.9 64.5 %copy-start.2 = (bf16[1,2,16,36,256]{4,2,3,1,0:T(8,128)(2,1)S(1)}, bf16[1,2,16,36,256]{4,2,3,1,0:T(8,128)(2,1)}, u32[]{:S(2)}) copy-start(bf16[1,2,16,36,256]{4,2,3,1,0:T(8,128)(2,1)} %param.8) | copy-start | bytes 1769476
  29.8 0.7 copy-start.12
  80.9 1.6 copy-start.1
  87.1 0.7 copy-start.15
  87.1 0.7 copy-start.16
  89.0 1.1 copy-start.5
  90.1 1.7 copy-start.3
  106.0 19.3 %collective-permute-start = (bf16[1,1,16,36,256]{4,3,2,1,0:T(8,128)(2,1)S(1)}, bf16[1,1,16,36,256]{4,3,2,1,0:T(8,128)(2,1)S(1)}, u32[]{:S(2)}, u32[]{:S(2)}) collective-permute-start(bf16[1,1,16,36,256]{4,3,2,1,0:T(8,128)(2,1)S(1)} %get-tuple-element.26), channel_id=1, source_target_pairs={{0,1},{1,2},{2,3},{3,4},{4,5},{5,6},{6,7},{7,8},{8,9},{9,10},{10,1... | collective-permute-start | bytes 884744 | tf_op jit(solution)/shard_map/ppermute | solution.py:20
  112.1 13.3 %copy-start.4 = (bf16[1,2,16,36,256]{4,2,3,1,0:T(8,128)(2,1)S(1)}, bf16[1,2,16,36,256]{4,2,3,1,0:T(8,128)(2,1)}, u32[]{:S(2)}) copy-start(bf16[1,2,16,36,256]{4,2,3,1,0:T(8,128)(2,1)} %param.8) | copy-start | bytes 1769476
  112.1 15.6 %collective-permute-start.1 = (bf16[1,1,16,36,256]{4,3,2,1,0:T(8,128)(2,1)S(1)}, bf16[1,1,16,36,256]{4,3,2,1,0:T(8,128)(2,1)S(1)}, u32[]{:S(2)}, u32[]{:S(2)}) collective-permute-start(bf16[1,1,16,36,256]{4,3,2,1,0:T(8,128)(2,1)S(1)} %get-tuple-element.27), channel_id=1, source_target_pairs={{1,0},{2,1},{3,2},{4,3},{5,4},{6,5},{7,6},{8,7},{9,8},{10,9},{11,1... | collective-permute-start | bytes 884744 | tf_op jit(solution)/shard_map/ppermute | solution.py:23
  125.3 1.2 copy-start.8
  127.7 0.7 copy-start.10
  129.7 1.1 copy-start.6
  129.7 289.0 %all-reduce.4.cloned.1.call-start = ((), (), s32[]{:S(2)}) async-start(), calls=%async_computation.3 | async-start | bytes 196608 | tf_op jit(solution)/shard_map/psum | solution.py:121
  131.7 99.9 %copy-start.11 = (bf16[1,1,16,36,256]{4,3,2,1,0:T(8,128)(2,1)S(1)}, bf16[1,1,16,36,256]{4,3,2,1,0:T(8,128)(2,1)}, u32[]{:S(2)}) copy-start(bf16[1,1,16,36,256]{4,3,2,1,0:T(8,128)(2,1)} %copy-done.10) | copy-start | bytes 884740
  231.6 20.5 %copy-start.9 = (bf16[1,1,16,36,256]{4,3,2,1,0:T(8,128)(2,1)S(1)}, bf16[1,1,16,36,256]{4,3,2,1,0:T(8,128)(2,1)}, u32[]{:S(2)}) copy-start(bf16[1,1,16,36,256]{4,3,2,1,0:T(8,128)(2,1)} %copy-done.8) | copy-start | bytes 884740
  254.3 164.3 %copy-start.7 = (f32[96,256]{1,0:T(8,128)S(1)}, f32[96,256]{1,0:T(8,128)}, u32[]{:S(2)}) copy-start(f32[96,256]{1,0:T(8,128)} %param.9) | copy-start | bytes 294916
  254.3 164.3 %copy-start.13 = (f32[96,256]{1,0:T(8,128)S(1)}, f32[96,256]{1,0:T(8,128)}, u32[]{:S(2)}) copy-start(f32[96,256]{1,0:T(8,128)} %param.10) | copy-start | bytes 294916
  254.4 164.3 %copy-start.14 = (f32[96,256]{1,0:T(8,128)S(1)}, f32[96,256]{1,0:T(8,128)}, u32[]{:S(2)}) copy-start(f32[96,256]{1,0:T(8,128)} %param.11) | copy-start | bytes 294916
Sparse Core Ops, SparseCore 0:
  10.7 70.1 all-gather.1
  129.8 122.2 reduce-scatter.1
  255.0 163.6 all-reduce.3
where the time goes:
time: 427 us
  waiting for transfers between devices  255 us (60%)
  blocking collectives  98.4 us (23%)
  matrix products  29.6 us (7%)
  between operations  14.1 us (3%)
  starting transfers between devices  12.7 us (3%)
  local copies, waits for them, and re-layouts  9.06 us (2%)
  other arithmetic  7.8 us (2%)
    psum x1, waiting for transfers between devices, shards(): gradient = lax.psum(row_block, 'tm')  163 us
    psum x1, blocking collectives, shards(): norm_grads = lax.psum(jnp.stack([gain_grad, bias_grad]), ('blk', 'tm'))  98.4 us
    all_gather x1, waiting for transfers between devices, shards(): lax.all_gather(conv_master.astype(jnp.bfloat16), 'blk', axis=0, tiled=True)  50.4 us
    ppermute x2, waiting for transfers between devices, extended(): lax.ppermute(lax.slice_in_dim(block, block.shape[dim] - width, None, axis...  22.2 us
    reduce_scatter x1, waiting for transfers between devices, shards(): lax.psum_scatter(local_gradient, 'blk', scatter_dimension=0, tiled=True)  19.1 us
    ppermute x2, starting transfers between devices, extended(): lax.ppermute(lax.slice_in_dim(block, block.shape[dim] - width, None, axis...  9.9 us
    dot_general x9, matrix products, shards(): jnp.einsum('bfhwc,bfhwd->cd', window, space_grad, preferred_element_type=...  9.86 us
  transfers between devices with their start and end apart: 7, of which 5 were waited for; matrix products, arithmetic and copies ran while one was open for 4% of the time, Pallas kernels for 0%

commit v1 on v0

--- a/solution.py
+++ b/solution.py
@@ -118,7 +118,8 @@
     local_gradient = jnp.concatenate(spatial_grads + temporal_grads, axis=0)
     norm_grads = lax.psum(jnp.stack([gain_grad, bias_grad]), ("blk", "tm"))
     row_block = lax.psum_scatter(local_gradient, "blk", scatter_dimension=0, tiled=True)
-    gradient = lax.psum(row_block, "tm")
+    convert_yards_now = lambda work_x: lax.all_gather(work_x, "tm").sum(axis=0)
+    gradient = convert_yards_now(row_block)
     new_master, new_first, new_second = adam_update(
         gradient, conv_master, first_moment, second_moment
     )

time: 427 us -> 372 us (0.87)
  the two profiles are of different devices: /device:TPU:8 before, /device:TPU:1 now
where the time goes in v1:
time: 372 us
  waiting for transfers between devices  197 us (53%)
  blocking collectives  105 us (28%)
  matrix products  25.8 us (7%)
  between operations  14.1 us (4%)
  starting transfers between devices  12.6 us (3%)
  local copies, waits for them, and re-layouts  8.65 us (2%)
  other arithmetic  8.42 us (2%)
    reduce_scatter x1, waiting for transfers between devices, shards(): lax.psum_scatter(local_gradient, 'blk', scatter_dimension=0, tiled=True)  124 us
    psum x1, blocking collectives, shards(): norm_grads = lax.psum(jnp.stack([gain_grad, bias_grad]), ('blk', 'tm'))  105 us
    all_gather x1, waiting for transfers between devices, shards(): lax.all_gather(conv_master.astype(jnp.bfloat16), 'blk', axis=0, tiled=True)  61.3 us
    ppermute x2, waiting for transfers between devices, extended(): lax.ppermute(lax.slice_in_dim(block, block.shape[dim] - width, None, axis...  12.1 us
    dot_general x9, matrix products, shards(): jnp.einsum('bfhwc,bfhwd->cd', window, space_grad, preferred_element_type=...  9.87 us
    ppermute x2, starting transfers between devices, extended(): lax.ppermute(lax.slice_in_dim(block, block.shape[dim] - width, None, axis...  9.8 us
  transfers between devices with their start and end apart: 7, of which 4 were waited for; matrix products, arithmetic and copies ran while one was open for 3% of the time, Pallas kernels for 0%

profile of v1, /device:TPU:1, one launch (start us, length us, event | category | flops | bytes accessed | tf_op | source)
XLA Modules:
  0.0 371.6 jit_solution(16759843771920146645)
XLA Ops:
  7.2 1.5 convert_element_type.38
  8.8 1.3 copy.26
  10.1 0.8 fusion.179
  10.9 5.5 %collective-permute-start.3 = (bf16[1,1,16,36,256]{4,3,2,1,0:T(8,128)(2,1)S(1)}, bf16[1,1,16,36,256]{4,3,2,1,0:T(8,128)(2,1)S(1)}, u32[]{:S(2)}, u32[]{:S(2)}) collective-permute-start(bf16[1,1,16,36,256]{4,3,2,1,0:T(8,128)(2,1)S(1)} %get-tuple-element.25), channel_id=1, source_target_pairs={{0,1},{1,2},{2,3},{3,4},{4,5},{5,6},{6,7},{7,8},{8,9},{9,10},{10,1... | collective-permute-start | bytes 884744 | tf_op jit(solution)/shard_map/ppermute | solution.py:20
  16.4 1.3 collective-permute-start.2
  18.9 2.1 collective-permute-done.3
  21.0 0.7 copy-done.12
  21.7 61.3 %all-gather.4.cloned.1.call-done = bf16[3072,256]{1,0:T(8,128)(2,1)} async-done(((bf16[96,256]{1,0:T(8,128)(2,1)}), bf16[3072,256]{1,0:T(8,128)(2,1)}) %all-gather.4.cloned.1.call-update) | async-done | bytes 1572880 | tf_op jit(solution)/shard_map/all_gather | solution.py:52
  83.1 1.5 fusion.51
  84.6 0.4 fusion.114
  85.1 1.3 fusion.9
  86.4 0.4 fusion.66
  87.2 0.4 convolution_add_fusion.6
  87.6 0.4 convolution_add_fusion.5
  88.4 0.4 convolution_add_fusion.3
  88.8 0.4 convolution_add_fusion.2
  89.9 1.2 fusion.26
  91.1 1.1 copy-done.5
  92.2 0.5 fusion.37
  93.9 3.0 fusion.14
  96.9 1.1 fusion.49
  98.0 1.1 fusion.48
  99.0 1.1 fusion.47
  100.1 1.1 fusion.46
  101.2 1.1 fusion.45
  102.3 1.1 fusion.44
  103.4 1.1 fusion.43
  105.6 0.4 convolution_add_fusion.15
  106.8 0.4 convolution_add_fusion.12
  107.2 0.5 convolution_add_fusion.11
  107.7 0.4 fusion.10
  108.1 4.3 %collective-permute-start = (bf16[1,1,16,36,256]{4,3,2,1,0:T(8,128)(2,1)S(1)}, bf16[1,1,16,36,256]{4,3,2,1,0:T(8,128)(2,1)S(1)}, u32[]{:S(2)}, u32[]{:S(2)}) collective-permute-start(bf16[1,1,16,36,256]{4,3,2,1,0:T(8,128)(2,1)S(1)} %get-tuple-element.26), channel_id=1, source_target_pairs={{0,1},{1,2},{2,3},{3,4},{4,5},{5,6},{6,7},{7,8},{8,9},{9,10},{10,1... | collective-permute-start | bytes 884744 | tf_op jit(solution)/shard_map/ppermute | solution.py:20
  112.5 1.1 fusion.42
  113.6 1.4 collective-permute-start.1
  115.0 1.1 fusion.41
  116.1 10.0 %collective-permute-done = bf16[1,1,16,36,256]{4,3,2,1,0:T(8,128)(2,1)S(1)} collective-permute-done((bf16[1,1,16,36,256]{4,3,2,1,0:T(8,128)(2,1)S(1)}, bf16[1,1,16,36,256]{4,3,2,1,0:T(8,128)(2,1)S(1)}, u32[]{:S(2)}, u32[]{:S(2)}) %collective-permute-start) | collective-permute-done | bytes 294944 | tf_op jit(solution)/shard_map/ppermute | solution.py:20
  126.1 1.2 fusion.40
  127.3 1.1 fusion.39
  128.5 0.7 copy-done.10
  129.2 1.2 fusion.38
  130.5 123.5 %reduce-scatter.2.cloned.1.call-done = f32[96,256]{1,0:T(8,128)} async-done(((f32[3072,256]{1,0:T(8,128)}), f32[96,256]{1,0:T(8,128)}) %reduce-scatter.2.cloned.1.call-update) | async-done | bytes 98320 | tf_op jit(solution)/shard_map/reduce_scatter | solution.py:120
  254.1 0.9 copy.36
  255.0 104.9 %psum.7 = f32[2,256]{1,0:T(2,128)} all-reduce(f32[2,256]{1,0:T(2,128)S(1)} %pad_maximum_fusion.4), channel_id=1, replica_groups=mesh['blk'=32,'tm'=16] {'blk','tm'}, use_global_device_ids=true, to_apply=%region_14.15 | all-reduce | flops 512 | bytes 4096 | tf_op jit(solution)/shard_map/psum | solution.py:119
  360.7 0.6 copy-done.9
  361.3 0.6 fusion.11
  361.9 0.9 copy.35
  362.8 1.5 reduce_sum.138
  364.4 0.7 multiply_subtract_fusion
  (76 shorter events, 6.6 us)
Async XLA Ops:
  7.2 75.9 %all-gather.4.cloned.1.call-start = ((), (), s32[]{:S(2)}) async-start(), calls=%async_computation.1 | async-start | bytes 1622016 | tf_op jit(solution)/shard_map/all_gather | solution.py:52
  8.7 8.9 %copy-start = (bf16[1,2,16,36,256]{4,2,3,1,0:T(8,128)(2,1)S(1)}, bf16[1,2,16,36,256]{4,2,3,1,0:T(8,128)(2,1)}, u32[]{:S(2)}) copy-start(bf16[1,2,16,36,256]{4,2,3,1,0:T(8,128)(2,1)} %param.7) | copy-start | bytes 1769476
  8.8 245.3 %reduce-scatter.2.cloned.1.call-start = ((), (), s32[]{:S(2)}) async-start(), calls=%async_computation.2 | async-start | bytes 3244032 | tf_op jit(solution)/shard_map/reduce_scatter | solution.py:120
  10.9 10.1 %collective-permute-start.3 = (bf16[1,1,16,36,256]{4,3,2,1,0:T(8,128)(2,1)S(1)}, bf16[1,1,16,36,256]{4,3,2,1,0:T(8,128)(2,1)S(1)}, u32[]{:S(2)}, u32[]{:S(2)}) collective-permute-start(bf16[1,1,16,36,256]{4,3,2,1,0:T(8,128)(2,1)S(1)} %get-tuple-element.25), channel_id=1, source_target_pairs={{0,1},{1,2},{2,3},{3,4},{4,5},{5,6},{6,7},{7,8},{8,9},{9,10},{10,1... | collective-permute-start | bytes 884744 | tf_op jit(solution)/shard_map/ppermute | solution.py:20
  16.4 68.7 %collective-permute-start.2 = (bf16[1,1,16,36,256]{4,3,2,1,0:T(8,128)(2,1)}, bf16[1,1,16,36,256]{4,3,2,1,0:T(8,128)(2,1)}, u32[]{:S(2)}, u32[]{:S(2)}) collective-permute-start(bf16[1,1,16,36,256]{4,3,2,1,0:T(8,128)(2,1)} %get-tuple-element.24), channel_id=1, source_target_pairs={{1,0},{2,1},{3,2},{4,3},{5,4},{6,5},{7,6},{8,7},{9,8},{10,9},{11,1... | collective-permute-start | bytes 884744 | tf_op jit(solution)/shard_map/ppermute | solution.py:23
  18.5 66.1 %copy-start.2 = (bf16[1,2,16,36,256]{4,2,3,1,0:T(8,128)(2,1)S(1)}, bf16[1,2,16,36,256]{4,2,3,1,0:T(8,128)(2,1)}, u32[]{:S(2)}) copy-start(bf16[1,2,16,36,256]{4,2,3,1,0:T(8,128)(2,1)} %param.8) | copy-start | bytes 1769476
  21.0 0.7 copy-start.12
  83.1 1.6 copy-start.1
  89.2 0.7 copy-start.15
  89.2 0.7 copy-start.16
  91.1 1.1 copy-start.5
  92.2 1.7 copy-start.3
  108.1 18.0 %collective-permute-start = (bf16[1,1,16,36,256]{4,3,2,1,0:T(8,128)(2,1)S(1)}, bf16[1,1,16,36,256]{4,3,2,1,0:T(8,128)(2,1)S(1)}, u32[]{:S(2)}, u32[]{:S(2)}) collective-permute-start(bf16[1,1,16,36,256]{4,3,2,1,0:T(8,128)(2,1)S(1)} %get-tuple-element.26), channel_id=1, source_target_pairs={{0,1},{1,2},{2,3},{3,4},{4,5},{5,6},{6,7},{7,8},{8,9},{9,10},{10,1... | collective-permute-start | bytes 884744 | tf_op jit(solution)/shard_map/ppermute | solution.py:20
  113.6 12.5 %copy-start.4 = (bf16[1,2,16,36,256]{4,2,3,1,0:T(8,128)(2,1)S(1)}, bf16[1,2,16,36,256]{4,2,3,1,0:T(8,128)(2,1)}, u32[]{:S(2)}) copy-start(bf16[1,2,16,36,256]{4,2,3,1,0:T(8,128)(2,1)} %param.8) | copy-start | bytes 1769476
  113.6 14.9 %collective-permute-start.1 = (bf16[1,1,16,36,256]{4,3,2,1,0:T(8,128)(2,1)S(1)}, bf16[1,1,16,36,256]{4,3,2,1,0:T(8,128)(2,1)S(1)}, u32[]{:S(2)}, u32[]{:S(2)}) collective-permute-start(bf16[1,1,16,36,256]{4,3,2,1,0:T(8,128)(2,1)S(1)} %get-tuple-element.27), channel_id=1, source_target_pairs={{1,0},{2,1},{3,2},{4,3},{5,4},{6,5},{7,6},{8,7},{9,8},{10,9},{11,1... | collective-permute-start | bytes 884744 | tf_op jit(solution)/shard_map/ppermute | solution.py:23
  126.1 1.2 copy-start.8
  128.5 0.7 copy-start.10
  130.4 123.6 %copy-start.6 = (bf16[1,2,16,36,256]{4,3,2,1,0:T(8,128)(2,1)S(1)}, bf16[1,2,16,36,256]{4,3,2,1,0:T(8,128)(2,1)}, u32[]{:S(2)}) copy-start(bf16[1,2,16,36,256]{4,3,2,1,0:T(8,128)(2,1)} %get-tuple-element.28) | copy-start | bytes 1769476
  130.5 232.4 %all-gather.6.cloned.1.call-start = ((), (), s32[]{:S(2)}) async-start(), calls=%async_computation.3 | async-start | bytes 1671168 | tf_op jit(solution)/shard_map/all_gather | solution.py:121
  255.0 105.3 %copy-start.11 = (bf16[1,1,16,36,256]{4,3,2,1,0:T(8,128)(2,1)S(1)}, bf16[1,1,16,36,256]{4,3,2,1,0:T(8,128)(2,1)}, u32[]{:S(2)}) copy-start(bf16[1,1,16,36,256]{4,3,2,1,0:T(8,128)(2,1)} %copy-done.10) | copy-start | bytes 884740
  360.3 1.0 copy-start.9
  361.9 2.5 copy-start.7
  361.9 2.5 copy-start.13
  361.9 2.5 copy-start.14
Sparse Core Ops, SparseCore 0:
  10.7 72.3 all-gather.3
  130.6 123.4 reduce-scatter.1
  257.2 83.4 all-gather.5
